TPU v7x, 32 devices: a whole 2x2x4 slice. The times are simulated.
32 devices in a mesh: wide: 8 (over z, y), lev: 4 (over x, core).
Axes of the slice: x: 2, y: 2, z: 4, core: 2. Of those that a mesh axis runs over, the one named last changes fastest.
Arguments:
- state_field: float32 [12, 1472, 1472], P('lev', 'wide'), may hold values from -8 to 8
- to_modes: float32 [12, 12], replicated, may hold values from -4 to 4
- from_modes: float32 [12, 12], replicated, may hold values from -4 to 4, as said below
- mode_depth: float32 [12], replicated, may hold values from 0.1 to 2000
Outputs:
- updated_field: float32 [12, 1472, 1472], P('lev', 'wide')
Inputs may be any that keep to these rules, and one draw needn't show every extreme that they name: `from_modes`: the inverse of to_modes.
All inputs are finite; a program needn't handle non-finite values.
Results may differ from a plain program's by a relative error of at most 0.000094.
Values sent between devices are 32-bit elements; how exact they have to be, the bound alone decides.
No kernel may reach another device: no remote copies, remote signals or barrier semaphores. Data moves between devices by JAX's collectives and lax.ppermute only.
A program may use at most 64 MiB of HBM per device.

v0:
```python
import math
import jax
import jax.numpy as jnp
from jax import lax
from jax.sharding import PartitionSpec as P

I = 1472
E = 64
KT = 512
highest = lax.Precision.HIGHEST


def spread(block, axis, owner):
    block = jnp.where(lax.axis_index(axis) == owner, block, jnp.zeros_like(block))
    return lax.psum(block, axis)


def blend_weights(fraction):
    square = fraction * fraction
    cubed = square * fraction
    return (
        2.0 * cubed - 3.0 * square + 1.0,
        cubed - 2.0 * square + fraction,
        -2.0 * cubed + 3.0 * square,
        cubed - square,
    )


def hermite_mix(start_val, start_slope, end_val, end_slope, weights):
    return (
        weights[0] * end_val
        + weights[1] * end_slope
        + weights[2] * start_val
        + weights[3] * start_slope
    )


def extend_cols(sub_block, extra):
    fraction = (jnp.arange(extra, dtype=jnp.float32) + 1.0) / (extra + 1.0)
    weights = blend_weights(fraction)
    end_val = sub_block[..., -1:]
    end_slope = sub_block[..., -1:] - sub_block[..., -2:-1]
    start_val = sub_block[..., :1]
    start_slope = sub_block[..., 1:2] - sub_block[..., :1]
    added = hermite_mix(start_val, start_slope, end_val, end_slope, weights)
    return jnp.concatenate([sub_block, added], axis=-1)


def laplace(waves, length):
    sines = jnp.sin(math.pi / length * waves.astype(jnp.float32))
    return 4.0 * sines * sines


def cas_table(positions, waves, length):
    product = positions[:, None] * waves[None, :] % length
    phase_angle = 2.0 * math.pi / length * product.astype(jnp.float32)
    return jnp.cos(phase_angle) + jnp.sin(phase_angle)


def wave_numbers(amount, length, bound):
    indices = jnp.arange(amount, dtype=jnp.int32)
    waves = jnp.where(indices < bound, indices, length - 2 * bound + 1 + indices)
    live_mask = indices < 2 * bound - 1
    waves = jnp.where(live_mask, waves, 0)
    magnitude = jnp.minimum(waves, length - waves)
    return (waves, live_mask.astype(jnp.float32), magnitude)


def shards(state_field, to_modes, from_modes, mode_depth):
    wide_count = lax.axis_size("wide")
    wide_index = lax.axis_index("wide")
    lev_index = lax.axis_index("lev")
    levels, row_count, col_count = state_field.shape
    length = I + E
    ext_count = E // wide_count
    row_total = row_count + ext_count
    head_strip = spread(state_field[:, :2], "wide", 0)
    tail_strip = spread(state_field[:, row_count - 2 :], "wide", wide_count - 1)
    ext_slot = (wide_count - wide_index) % wide_count
    row_ids = ext_slot * ext_count + jnp.arange(ext_count, dtype=jnp.int32)
    fraction = (row_ids.astype(jnp.float32) + 1.0) / (E + 1.0)
    weights = tuple((weight[:, None] for weight in blend_weights(fraction)))
    end_val = tail_strip[:, 1:2]
    end_slope = tail_strip[:, 1:2] - tail_strip[:, 0:1]
    start_val = head_strip[:, 0:1]
    start_slope = head_strip[:, 1:2] - head_strip[:, 0:1]
    ext_block = hermite_mix(start_val, start_slope, end_val, end_slope, weights)
    stacked = jnp.concatenate([state_field, ext_block], axis=1)
    widened = extend_cols(stacked, E)
    spec_count = 2 * KT
    waves, live_mask, magnitude = wave_numbers(spec_count, length, KT)
    lap_all = laplace(waves, length)
    positions = jnp.arange(length, dtype=jnp.int32)
    forward_x = cas_table(positions, waves, length) * live_mask[None, :]
    row_owner = positions // row_total
    local_row = positions % row_total
    ext_owner = (wide_count - row_owner) % wide_count
    row_pos = jnp.where(
        local_row < row_count,
        row_owner * row_count + local_row,
        I + ext_owner * ext_count + local_row - row_count,
    )
    forward_y = cas_table(row_pos, waves, length) * live_mask[None, :]
    inverse_y = forward_y.T / length
    inverse_x = forward_x[:I].T / length
    col_span = spec_count // wide_count
    col_start = wide_index * col_span
    spec_x = jnp.einsum("irn,nc->irc", widened, forward_x, precision=highest)
    spectrum = jnp.einsum(
        "irc,rk->ick",
        lax.all_to_all(spec_x, "wide", split_axis=2, concat_axis=1, tiled=True),
        forward_y,
        precision=highest,
    )
    lev_start = lev_index * levels
    sub_block = lax.dynamic_slice(to_modes, (0, lev_start), (lax.axis_size("lev") * levels, levels))
    mode_values = lax.psum_scatter(
        jnp.einsum("ml,lck->mck", sub_block, spectrum, precision=highest),
        "lev",
        scatter_dimension=0,
        tiled=True,
    )
    lap_cols = lax.dynamic_slice_in_dim(lap_all, col_start, col_span)
    mag_cols = lax.dynamic_slice_in_dim(magnitude, col_start, col_span)
    live_cols = lax.dynamic_slice_in_dim(live_mask, col_start, col_span)
    inside = (
        mag_cols[:, None] * mag_cols[:, None] + magnitude[None, :] * magnitude[None, :] < KT * KT
    )
    keep_mask = live_cols[:, None] * live_mask[None, :] * inside.astype(jnp.float32)
    keep_mask, lap_sum = (keep_mask, lap_cols[:, None] + lap_all[None, :])
    mode_rates = lax.dynamic_slice_in_dim(mode_depth, lev_start, levels)
    solved = mode_values * keep_mask / (1.0 + mode_rates[:, None, None] * lap_sum)
    shard_piece = lax.all_gather(solved, "lev", axis=0, tiled=True)
    sub_block = lax.dynamic_slice(from_modes, (lev_start, 0), (levels, shard_piece.shape[0]))
    mixed_levels = jnp.einsum("lm,mck->lck", sub_block, shard_piece, precision=highest)
    rows_back = jnp.einsum("ick,kr->icr", mixed_levels, inverse_y, precision=highest)
    return jnp.einsum(
        "icr,cn->irn",
        lax.all_to_all(rows_back, "wide", split_axis=2, concat_axis=1, tiled=True)[
            :, :, :row_count
        ],
        inverse_x,
        precision=highest,
    )


def solution(mesh):
    placed = (P("lev", "wide", None), P(), P(), P())
    return jax.shard_map(
        shards, mesh=mesh, in_specs=placed, out_specs=P("lev", "wide", None), check_vma=False
    )
```

profile of v0, /device:TPU:0, one launch (start us, length us, event | category | flops | bytes accessed | tf_op | source)
XLA Modules:
  0.0 513.1 jit_solution(13678874333688489325)
XLA Ops:
  6.5 1.8 slice_select_fusion.1
  8.5 74.6 %all-reduce.3.cloned.1.call-done = (f32[3,2,1472]{2,1,0:T(2,128)}, f32[3,2,1472]{2,1,0:T(2,128)}) async-done(((f32[3,2,1472]{2,1,0:T(2,128)}, f32[3,2,1472]{2,1,0:T(2,128)}), (f32[3,2,1472]{2,1,0:T(2,128)}, f32[3,2,1472]{2,1,0:T(2,128)})) %all-reduce.3.cloned.1.call-update) | async-done | bytes 70672 | tf_op jit(solution)/shard_map/psum | solution.py:15
  83.1 0.9 fusion.107
  84.2 2.0 fusion.66
  87.0 38.5 %fusion.12 = f32[3,192,1024]{2,1,0:T(8,128)S(1)} fusion(f32[1024]{0:T(1024)S(1)} %fusion.85, s32[1024]{0:T(1024)S(1)} %fusion.86, f32[3,192,1536]{2,1,0:T(8,128)S(1)} %fusion.124), kind=kOutput, calls=%fused_computation.15 | convolution fusion | flops 10888937472 | bytes 5906432 | tf_op jit(solution)/shard_map/irn,nc->irc/dot_general | solution.py:108
  125.5 3.2 copy.32
  128.7 4.8 all-to-all-start
  133.5 91.4 %all-to-all-done = f32[3,192,1024]{1,0,2:T(4,128)} async-done(((f32[3,192,1024]{1,0,2:T(4,128)}), f32[3,192,1024]{1,0,2:T(4,128)}, u32[]{:S(2)}, u32[]{:S(2)}) %all-to-all-start) | async-done | bytes 2359328 | tf_op jit(solution)/shard_map/all_to_all | solution.py:111
  224.9 3.4 copy.45
  228.3 41.6 %fusion.10 = f32[3,128,1024]{2,1,0:T(8,128)S(1)} fusion(f32[3,1536,128]{2,1,0:T(8,128)S(1)} %bitcast.57, s32[1536]{0:T(1024)S(1)} %fusion.78, f32[1024]{0:T(1024)S(1)} %fusion.85, s32[1024]{0:T(1024)S(1)} %fusion.86), kind=kOutput, calls=%fused_computation.13 | convolution fusion | flops 7265058816 | bytes 3946496 | tf_op jit(solution)/shard_map/irc,rk->ick/dot_general | solution.py:109
  270.0 7.3 %fusion.59 = f32[12,128,1024]{2,0,1:T(8,128)S(1)} fusion(f32[3,128,1024]{2,1,0:T(8,128)S(1)} %fusion.10, f32[12,12]{1,0:T(8,128)S(1)} %copy-done, s32[]{:T(128)S(6)} %select_n.144), kind=kOutput, calls=%fused_computation.63 | convolution fusion | flops 56623104 | bytes 7864900 | tf_op jit(solution)/shard_map/ml,lck->mck/dot_general | solution.py:118
  277.3 6.3 %copy.37 = f32[12,128,1024]{2,1,0:T(8,128)} copy(f32[12,128,1024]{2,0,1:T(8,128)S(1)} %fusion.59) | data formatting | bytes 12582912 | tf_op jit(solution)/shard_map/ml,lck->mck/dot_general | solution.py:118
  284.7 56.9 %reduce-scatter.2.cloned.1.call-done = f32[3,128,1024]{2,1,0:T(8,128)} async-done(((f32[12,128,1024]{2,1,0:T(8,128)}), f32[3,128,1024]{2,1,0:T(8,128)}) %reduce-scatter.2.cloned.1.call-update) | async-done | bytes 1572880 | tf_op jit(solution)/shard_map/reduce_scatter | solution.py:117
  341.7 2.9 add_divide_fusion
  344.7 27.9 %fusion.122 = f32[1024,1536,1]{1,0,2:T(8,128)} fusion(f32[1024]{0:T(1024)S(1)} %fusion.85, s32[1024]{0:T(1024)S(1)} %fusion.86, s32[1536]{0:T(1024)S(1)} %fusion.78), kind=kLoop, calls=%fused_computation.12.clone.1 | loop fusion | flops 18874368 | bytes 6305792 | tf_op jit(solution)/shard_map/ick,kr->icr/dot_general | solution.py:136
  372.5 18.7 %all-gather.2.cloned.1.call-done = f32[12,128,1024]{2,1,0:T(8,128)} async-done(((f32[3,128,1024]{2,1,0:T(8,128)}), f32[12,128,1024]{2,1,0:T(8,128)}) %all-gather.2.cloned.1.call-update) | async-done | bytes 6291472 | tf_op jit(solution)/shard_map/all_gather | solution.py:133
  391.2 11.3 %fusion = f32[3,128,1024]{2,0,1:T(4,128)S(1)} fusion(f32[12,128,1024]{2,1,0:T(8,128)} %all-gather.2.cloned.1.call-done, f32[12,12]{1,0:T(8,128)} %param.6, s32[]{:T(128)S(6)} %select_n.144), kind=kOutput, calls=%fused_computation.3 | convolution fusion | flops 56623104 | bytes 7866372 | tf_op jit(solution)/shard_map/lm,mck->lck/dot_general | solution.py:135
  402.5 8.6 %fusion.8 = f32[3,128,1536]{2,1,0:T(8,128)S(1)} fusion(f32[3,128,1024]{2,0,1:T(4,128)S(1)} %fusion, f32[1024,1536,1]{1,0,2:T(8,128)S(1)} %copy-done.2), kind=kOutput, calls=%fused_computation.11 | convolution fusion | flops 7247757312 | bytes 10223616 | tf_op jit(solution)/shard_map/ick,kr->icr/dot_general | solution.py:136
  411.1 2.7 copy.40
  413.9 5.8 %all-to-all-start.1 = ((f32[3,128,1536]{1,0,2:T(4,128)}), f32[3,128,1536]{1,0,2:T(4,128)S(1)}, u32[]{:S(2)}, u32[]{:S(2)}) async-start(f32[3,128,1536]{1,0,2:T(4,128)} %copy.40), calls=%async_computation.2 | async-start | bytes 6291456 | tf_op jit(solution)/shard_map/all_to_all | solution.py:139
  419.6 27.2 %add_multiply_fusion = f32[1536,1024]{1,0:T(8,128)} fusion(f32[1024]{0:T(1024)S(1)} %fusion.85, s32[1024]{0:T(1024)S(1)} %fusion.86), kind=kLoop, calls=%fused_computation.32 | loop fusion | flops 17301504 | bytes 6299648 | tf_op jit(solution)/shard_map/mul | solution.py:94
  446.8 43.9 %all-to-all-done.1 = f32[3,128,1536]{1,0,2:T(4,128)S(1)} async-done(((f32[3,128,1536]{1,0,2:T(4,128)}), f32[3,128,1536]{1,0,2:T(4,128)S(1)}, u32[]{:S(2)}, u32[]{:S(2)}) %all-to-all-start.1) | async-done | bytes 2359328 | tf_op jit(solution)/shard_map/all_to_all | solution.py:139
  491.2 2.3 copy-done.3
  493.5 12.7 %fusion.37 = f32[3,184,1472]{2,1,0:T(8,128)} fusion(f32[1536,1024]{1,0:T(8,128)S(1)} %copy-done.3, f32[3,1024,192]{1,2,0:T(8,128)S(1)} %bitcast.56), kind=kOutput, calls=%fused_computation.41 | convolution fusion | flops 9986048000 | bytes 11540480 | tf_op jit(solution)/shard_map/icr,cn->irn/dot_general | solution.py:137
  (42 shorter events, 2.6 us)
Async XLA Ops:
  6.5 263.4 %copy-start = (f32[12,12]{1,0:T(8,128)S(1)}, f32[12,12]{1,0:T(8,128)}, u32[]{:S(2)}) copy-start(f32[12,12]{1,0:T(8,128)} %param.5) | copy-start | bytes 1732
  6.5 80.1 %copy-start.4 = (f32[3,184,1472]{2,1,0:T(8,128)S(1)}, f32[3,184,1472]{2,1,0:T(8,128)}, u32[]{:S(2)}) copy-start(f32[3,184,1472]{2,1,0:T(8,128)} %param.4) | copy-start | bytes 9750532
  6.5 76.5 %all-reduce.3.cloned.1.call-start = ((), (), s32[]{:S(2)}) async-start(), calls=%async_computation.5 | async-start | bytes 147456 | tf_op jit(solution)/shard_map/psum | solution.py:15
  128.7 96.2 %all-to-all-start = ((f32[3,192,1024]{1,0,2:T(4,128)}), f32[3,192,1024]{1,0,2:T(4,128)}, u32[]{:S(2)}, u32[]{:S(2)}) async-start(f32[3,192,1024]{1,0,2:T(4,128)} %copy.32), calls=%async_computation | async-start | bytes 8388608 | tf_op jit(solution)/shard_map/all_to_all | solution.py:111
  133.5 208.2 %reduce-scatter.2.cloned.1.call-start = ((), (), s32[]{:S(2)}) async-start(), calls=%async_computation.3 | async-start | bytes 7864320 | tf_op jit(solution)/shard_map/reduce_scatter | solution.py:117
  283.6 0.7 copy-start.5
  283.6 107.5 %all-gather.2.cloned.1.call-start = ((), (), s32[]{:S(2)}) async-start(), calls=%async_computation.4 | async-start | bytes 7864320 | tf_op jit(solution)/shard_map/all_gather | solution.py:133
  391.2 11.4 %copy-start.2 = (f32[1024,1536,1]{1,0,2:T(8,128)S(1)}, f32[1024,1536,1]{1,0,2:T(8,128)}, u32[]{:S(2)}) copy-start(f32[1024,1536,1]{1,0,2:T(8,128)} %fusion.122) | copy-start | bytes 18874372
  413.9 76.8 %all-to-all-start.1 = ((f32[3,128,1536]{1,0,2:T(4,128)}), f32[3,128,1536]{1,0,2:T(4,128)S(1)}, u32[]{:S(2)}, u32[]{:S(2)}) async-start(f32[3,128,1536]{1,0,2:T(4,128)} %copy.40), calls=%async_computation.2 | async-start | bytes 6291456 | tf_op jit(solution)/shard_map/all_to_all | solution.py:139
  490.7 2.8 copy-start.3
  490.9 15.3 %copy-start.1 = (f32[12,12]{1,0:T(8,128)S(1)}, f32[12,12]{1,0:T(8,128)}, u32[]{:S(2)}) copy-start(f32[12,12]{1,0:T(8,128)} %param.5) | copy-start | bytes 1732
Sparse Core Ops, SparseCore 0:
  10.8 72.1 all-reduce.2
  283.8 57.8 reduce-scatter.1
  344.8 46.3 all-gather.1
where the time goes:
time: 522 us; the launch traced here: 513 us
  waiting for transfers between devices  286 us (55%)
  matrix products  120 us (23%)
  other arithmetic  64.1 us (12%)
  local copies, waits for them, and re-layouts  19 us (4%)
  between operations  13.7 us (3%)
  starting transfers between devices  10.6 us (2%)
    all_to_all x1, waiting for transfers between devices, shards(): lax.all_to_all(spec_x, 'wide', split_axis=2, concat_axis=1, tiled=True)  91.4 us
    psum x1, waiting for transfers between devices, spread(): return lax.psum(block, axis)  74.6 us
    reduce_scatter x1, waiting for transfers between devices, shards(): lax.psum_scatter(jnp.einsum('ml,lck->mck', sub_block, spectrum, precision...  56.9 us
    all_to_all x1, waiting for transfers between devices, shards(): lax.all_to_all(rows_back, 'wide', split_axis=2, concat_axis=1, tiled=True)  43.9 us
    dot_general x1, matrix products, shards(): jnp.einsum('irc,rk->ick', lax.all_to_all(spec_x, 'wide', split_axis=2, co...  41.6 us
    dot_general x1, matrix products, shards(): spec_x = jnp.einsum('irn,nc->irc', widened, forward_x, precision=highest)  38.5 us
    dot_general x1, other arithmetic, shards(): jnp.einsum('ick,kr->icr', mixed_levels, inverse_y, precision=highest)  27.9 us
    mul x1, other arithmetic, shards(): forward_x = cas_table(positions, waves, length) * live_mask[None, :]  27.2 us
  transfers between devices with their start and end apart: 5, of which 5 were waited for; matrix products, arithmetic and copies ran while one was open for 11% of the time, Pallas kernels for 0%

commit v1 on v0

--- a/solution.py
+++ b/solution.py
@@ -8,6 +8,12 @@
 E = 64
 KT = 512
 highest = lax.Precision.HIGHEST
+
+
+def trade_parts(array, axis, split, join):
+    pieces = jnp.split(array, lax.axis_size(axis), axis=split)
+    received = lax.all_to_all(jnp.stack(pieces), axis, 0, 0)
+    return jnp.concatenate(received, axis=join)
 
 
 def spread(block, axis, owner):
@@ -107,10 +113,7 @@
     col_start = wide_index * col_span
     spec_x = jnp.einsum("irn,nc->irc", widened, forward_x, precision=highest)
     spectrum = jnp.einsum(
-        "irc,rk->ick",
-        lax.all_to_all(spec_x, "wide", split_axis=2, concat_axis=1, tiled=True),
-        forward_y,
-        precision=highest,
+        "irc,rk->ick", trade_parts(spec_x, "wide", 2, 1), forward_y, precision=highest
     )
     lev_start = lev_index * levels
     sub_block = lax.dynamic_slice(to_modes, (0, lev_start), (lax.axis_size("lev") * levels, levels))

time: 522 us -> 483 us (0.925)
  waiting for transfers between devices: 286 us -> 246 us
    all_to_all x1, waiting for transfers between devices: 91.4 us -> 52 us  [trade_parts(): received = lax.all_to_all(jnp.stack(pieces), axis, 0, 0)]
    unnamed x16 -> x23, local copies, waits for them, and re-layouts: 2.72 us -> 8 us
  transfers between devices with their start and end apart: 5 -> 5, of which waited for: 5 -> 5; matrix products, arithmetic and copies ran while one was open for 11% -> 12% of each run, Pallas kernels for 0% -> 0%
where the time goes in v1:
time: 483 us; the launch traced here: 473 us
  waiting for transfers between devices  246 us (51%)
  matrix products  120 us (25%)
  other arithmetic  64.1 us (13%)
  local copies, waits for them, and re-layouts  18.7 us (4%)
  between operations  13.7 us (3%)
  starting transfers between devices  10.4 us (2%)
    psum x1, waiting for transfers between devices, spread(): return lax.psum(block, axis)  74.6 us
    reduce_scatter x1, waiting for transfers between devices, shards(): lax.psum_scatter(jnp.einsum('ml,lck->mck', sub_block, spectrum, precision...  56.9 us
    all_to_all x1, waiting for transfers between devices, trade_parts(): received = lax.all_to_all(jnp.stack(pieces), axis, 0, 0)  52 us
    all_to_all x1, waiting for transfers between devices, shards(): lax.all_to_all(rows_back, 'wide', split_axis=2, concat_axis=1, tiled=True)  43.9 us
    dot_general x1, matrix products, shards(): jnp.einsum('irc,rk->ick', trade_parts(spec_x, 'wide', 2, 1), forward_y, p...  41.9 us
    dot_general x1, matrix products, shards(): spec_x = jnp.einsum('irn,nc->irc', widened, forward_x, precision=highest)  38.5 us
    dot_general x1, other arithmetic, shards(): jnp.einsum('ick,kr->icr', mixed_levels, inverse_y, precision=highest)  27.9 us
    mul x1, other arithmetic, shards(): forward_x = cas_table(positions, waves, length) * live_mask[None, :]  27.2 us
  transfers between devices with their start and end apart: 5, of which 5 were waited for; matrix products, arithmetic and copies ran while one was open for 12% of the time, Pallas kernels for 0%

profile of v1, /device:TPU:0, one launch (start us, length us, event | category | flops | bytes accessed | tf_op | source)
XLA Modules:
  0.0 473.3 jit_solution(4524985406859621668)
XLA Ops:
  6.5 1.8 slice_select_fusion.1
  8.5 74.6 %all-reduce.3.cloned.1.call-done = (f32[3,2,1472]{2,1,0:T(2,128)}, f32[3,2,1472]{2,1,0:T(2,128)}) async-done(((f32[3,2,1472]{2,1,0:T(2,128)}, f32[3,2,1472]{2,1,0:T(2,128)}), (f32[3,2,1472]{2,1,0:T(2,128)}, f32[3,2,1472]{2,1,0:T(2,128)})) %all-reduce.3.cloned.1.call-update) | async-done | bytes 70672 | tf_op jit(solution)/shard_map/psum | solution.py:21
  83.1 0.9 fusion.115
  84.2 2.0 fusion.74
  87.0 38.5 %fusion.12 = f32[3,192,1024]{2,1,0:T(8,128)S(1)} fusion(f32[1024]{0:T(1024)S(1)} %fusion.93, s32[1024]{0:T(1024)S(1)} %fusion.94, f32[3,192,1536]{2,1,0:T(8,128)S(1)} %fusion.132), kind=kOutput, calls=%fused_computation.15 | convolution fusion | flops 10888937472 | bytes 5906432 | tf_op jit(solution)/shard_map/irn,nc->irc/dot_general | solution.py:114
  127.0 0.8 fusion.67
  127.7 0.8 fusion.66
  131.5 4.6 all-to-all-start
  136.2 52.0 %all-to-all-done = f32[8,3,192,128]{3,2,1,0:T(8,128)S(1)} async-done(((f32[8,3,192,128]{3,2,1,0:T(8,128)}), f32[8,3,192,128]{3,2,1,0:T(8,128)S(1)}, u32[]{:S(2)}, u32[]{:S(2)}) %all-to-all-start) | async-done | bytes 2359328 | tf_op jit(solution)/shard_map/all_to_all | solution.py:15
  188.3 41.9 %fusion.10 = f32[3,128,1024]{2,1,0:T(8,128)S(1)} fusion(f32[3,1536,128]{2,1,0:T(8,128)S(1)} %bitcast.87, s32[1536]{0:T(1024)S(1)} %fusion.86, f32[1024]{0:T(1024)S(1)} %fusion.93, s32[1024]{0:T(1024)S(1)} %fusion.94), kind=kOutput, calls=%fused_computation.13 | convolution fusion | flops 7265058816 | bytes 3946496 | tf_op jit(solution)/shard_map/irc,rk->ick/dot_general | solution.py:115
  230.3 7.3 %fusion.59 = f32[12,128,1024]{2,0,1:T(8,128)S(1)} fusion(f32[3,128,1024]{2,1,0:T(8,128)S(1)} %fusion.10, f32[12,12]{1,0:T(8,128)S(1)} %copy-done, s32[]{:T(128)S(6)} %select_n.144), kind=kOutput, calls=%fused_computation.63 | convolution fusion | flops 56623104 | bytes 7864900 | tf_op jit(solution)/shard_map/ml,lck->mck/dot_general | solution.py:121
  237.6 6.3 %copy.23 = f32[12,128,1024]{2,1,0:T(8,128)} copy(f32[12,128,1024]{2,0,1:T(8,128)S(1)} %fusion.59) | data formatting | bytes 12582912 | tf_op jit(solution)/shard_map/ml,lck->mck/dot_general | solution.py:121
  245.0 56.9 %reduce-scatter.2.cloned.1.call-done = f32[3,128,1024]{2,1,0:T(8,128)} async-done(((f32[12,128,1024]{2,1,0:T(8,128)}), f32[3,128,1024]{2,1,0:T(8,128)}) %reduce-scatter.2.cloned.1.call-update) | async-done | bytes 1572880 | tf_op jit(solution)/shard_map/reduce_scatter | solution.py:120
  301.9 2.9 add_divide_fusion
  304.9 27.9 %fusion.130 = f32[1024,1536,1]{1,0,2:T(8,128)} fusion(f32[1024]{0:T(1024)S(1)} %fusion.93, s32[1024]{0:T(1024)S(1)} %fusion.94, s32[1536]{0:T(1024)S(1)} %fusion.86), kind=kLoop, calls=%fused_computation.12.clone.1 | loop fusion | flops 18874368 | bytes 6305792 | tf_op jit(solution)/shard_map/ick,kr->icr/dot_general | solution.py:139
  332.8 18.7 %all-gather.2.cloned.1.call-done = f32[12,128,1024]{2,1,0:T(8,128)} async-done(((f32[3,128,1024]{2,1,0:T(8,128)}), f32[12,128,1024]{2,1,0:T(8,128)}) %all-gather.2.cloned.1.call-update) | async-done | bytes 6291472 | tf_op jit(solution)/shard_map/all_gather | solution.py:136
  351.4 11.3 %fusion = f32[3,128,1024]{2,0,1:T(4,128)S(1)} fusion(f32[12,128,1024]{2,1,0:T(8,128)} %all-gather.2.cloned.1.call-done, f32[12,12]{1,0:T(8,128)} %param.6, s32[]{:T(128)S(6)} %select_n.144), kind=kOutput, calls=%fused_computation.3 | convolution fusion | flops 56623104 | bytes 7866372 | tf_op jit(solution)/shard_map/lm,mck->lck/dot_general | solution.py:138
  362.8 8.6 %fusion.8 = f32[3,128,1536]{2,1,0:T(8,128)S(1)} fusion(f32[3,128,1024]{2,0,1:T(4,128)S(1)} %fusion, f32[1024,1536,1]{1,0,2:T(8,128)S(1)} %copy-done.2), kind=kOutput, calls=%fused_computation.11 | convolution fusion | flops 7247757312 | bytes 10223616 | tf_op jit(solution)/shard_map/ick,kr->icr/dot_general | solution.py:139
  371.4 2.7 copy.26
  374.1 5.8 %all-to-all-start.1 = ((f32[3,128,1536]{1,0,2:T(4,128)}), f32[3,128,1536]{1,0,2:T(4,128)S(1)}, u32[]{:S(2)}, u32[]{:S(2)}) async-start(f32[3,128,1536]{1,0,2:T(4,128)} %copy.26), calls=%async_computation.2 | async-start | bytes 6291456 | tf_op jit(solution)/shard_map/all_to_all | solution.py:142
  379.9 27.2 %add_multiply_fusion = f32[1536,1024]{1,0:T(8,128)} fusion(f32[1024]{0:T(1024)S(1)} %fusion.93, s32[1024]{0:T(1024)S(1)} %fusion.94), kind=kLoop, calls=%fused_computation.32 | loop fusion | flops 17301504 | bytes 6299648 | tf_op jit(solution)/shard_map/mul | solution.py:100
  407.1 43.9 %all-to-all-done.1 = f32[3,128,1536]{1,0,2:T(4,128)S(1)} async-done(((f32[3,128,1536]{1,0,2:T(4,128)}), f32[3,128,1536]{1,0,2:T(4,128)S(1)}, u32[]{:S(2)}, u32[]{:S(2)}) %all-to-all-start.1) | async-done | bytes 2359328 | tf_op jit(solution)/shard_map/all_to_all | solution.py:142
  451.4 2.3 copy-done.3
  453.7 12.7 %fusion.37 = f32[3,184,1472]{2,1,0:T(8,128)} fusion(f32[1536,1024]{1,0:T(8,128)S(1)} %copy-done.3, f32[3,1024,192]{1,2,0:T(8,128)S(1)} %bitcast.86), kind=kOutput, calls=%fused_computation.41 | convolution fusion | flops 9986048000 | bytes 11540480 | tf_op jit(solution)/shard_map/icr,cn->irn/dot_general | solution.py:140
  (49 shorter events, 7.4 us)
Async XLA Ops:
  6.5 223.7 %copy-start = (f32[12,12]{1,0:T(8,128)S(1)}, f32[12,12]{1,0:T(8,128)}, u32[]{:S(2)}) copy-start(f32[12,12]{1,0:T(8,128)} %param.5) | copy-start | bytes 1732
  6.5 80.1 %copy-start.4 = (f32[3,184,1472]{2,1,0:T(8,128)S(1)}, f32[3,184,1472]{2,1,0:T(8,128)}, u32[]{:S(2)}) copy-start(f32[3,184,1472]{2,1,0:T(8,128)} %param.4) | copy-start | bytes 9750532
  6.5 76.5 %all-reduce.3.cloned.1.call-start = ((), (), s32[]{:S(2)}) async-start(), calls=%async_computation.5 | async-start | bytes 147456 | tf_op jit(solution)/shard_map/psum | solution.py:21
  131.5 56.6 %all-to-all-start = ((f32[8,3,192,128]{3,2,1,0:T(8,128)}), f32[8,3,192,128]{3,2,1,0:T(8,128)S(1)}, u32[]{:S(2)}, u32[]{:S(2)}) async-start(f32[8,3,192,128]{3,2,1,0:T(8,128)} %fusion.62), calls=%async_computation | async-start | bytes 4718592 | tf_op jit(solution)/shard_map/all_to_all | solution.py:15
  136.1 165.8 %reduce-scatter.2.cloned.1.call-start = ((), (), s32[]{:S(2)}) async-start(), calls=%async_computation.3 | async-start | bytes 7864320 | tf_op jit(solution)/shard_map/reduce_scatter | solution.py:120
  243.9 0.7 copy-start.5
  243.9 107.5 %all-gather.2.cloned.1.call-start = ((), (), s32[]{:S(2)}) async-start(), calls=%async_computation.4 | async-start | bytes 7864320 | tf_op jit(solution)/shard_map/all_gather | solution.py:136
  351.4 11.4 %copy-start.2 = (f32[1024,1536,1]{1,0,2:T(8,128)S(1)}, f32[1024,1536,1]{1,0,2:T(8,128)}, u32[]{:S(2)}) copy-start(f32[1024,1536,1]{1,0,2:T(8,128)} %fusion.130) | copy-start | bytes 18874372
  374.1 76.8 %all-to-all-start.1 = ((f32[3,128,1536]{1,0,2:T(4,128)}), f32[3,128,1536]{1,0,2:T(4,128)S(1)}, u32[]{:S(2)}, u32[]{:S(2)}) async-start(f32[3,128,1536]{1,0,2:T(4,128)} %copy.26), calls=%async_computation.2 | async-start | bytes 6291456 | tf_op jit(solution)/shard_map/all_to_all | solution.py:142
  451.0 2.8 copy-start.3
  451.4 15.0 %copy-start.1 = (f32[12,12]{1,0:T(8,128)S(1)}, f32[12,12]{1,0:T(8,128)}, u32[]{:S(2)}) copy-start(f32[12,12]{1,0:T(8,128)} %param.5) | copy-start | bytes 1732
Sparse Core Ops, SparseCore 0:
  10.8 72.1 all-reduce.2
  244.1 57.8 reduce-scatter.1
  305.0 46.3 all-gather.1
